TPU v7x, 512 devices: a whole 4x8x8 slice. The times are simulated.
512 devices in a mesh: pole: 8 (over z_lo, core), row: 4 (over x), col: 16 (over y, z_hi).
Axes of the slice: x: 4, y: 8, z: 8 (z_hi: 2, z_lo: 4; z = z_hi * 4 + z_lo), core: 2. Of those that a mesh axis runs over, the one named last changes fastest.
Arguments:
- inverse_block: bfloat16 [8, 2, 16, 4, 64, 4096], P('pole', None, None, 'row', None, 'col'), may hold values from -5 to 5
- panels: bfloat16 [8, 3, 2, 16, 4, 64, 256], P('pole', None, None, 'col', 'row'), may hold values from -0.09375 to 0.09375
- panel_mask: int32 [3, 16, 4], P(None, 'col', 'row'), may hold values 0 or 1
- parent_panels: float32 [8, 2, 2, 256, 256], P('pole'), may hold values from -0.25 to 0.25
- diag_inverse: float32 [8, 3, 2, 256, 256], P('pole'), may hold values from -6 to 6
- pole_weights: float32 [8, 2], P('pole'), may hold values from 0.5 to 1.5
Outputs:
- density_panel: float32 [3, 16, 4, 64, 256], P(None, 'col', 'row', None, 'pole')
- density_diag: float32 [3, 256, 256], replicated
Inputs may be any that keep to these rules, and one draw needn't show every extreme that they name: panel_mask[k, a, b] is 1 where the block of 64 ancestor rows (a, b) of supernode k's factor panel may be nonzero, 0 where it is structurally zero.
All inputs are finite; a program needn't handle non-finite values.
Results may differ from a plain program's by a relative error of at most 0.0003.
Values may be sent and summed in bfloat16 or wider, within the bound.
A program may use at most 64 MiB of HBM per device.

v0:
```python
import jax
import jax.numpy as jnp
from jax import lax
from jax.sharding import Mesh
from jax.sharding import PartitionSpec as P

COL = ("col_0", "col_1")
POLE_ROW_COL = ("pole", "row", "col_0", "col_1")


def gather_axes(array, axes, dim):
    whole = array
    for number in range(len(axes) - 1, -1, -1):
        whole = lax.all_gather(whole, axes[number], axis=dim, tiled=True)
    return whole


def in_blocks(array, dim, devices):
    shape = array.shape
    pieces = array.reshape(*shape[:dim], devices, shape[dim] // devices, *shape[dim + 1 :])
    return jnp.moveaxis(pieces, dim, 0)


def summed_on_arrival(array, axis, dim):
    devices = lax.axis_size(axis)
    pieces = lax.all_to_all(in_blocks(array, dim, devices), axis, 0, 0, tiled=True)
    return jnp.sum(pieces, axis=0)


def matmul_high(left_side, right_side):
    return jnp.dot(
        left_side, right_side, precision=lax.Precision.HIGHEST, preferred_element_type=jnp.float32
    )


def complex_dot(left_real, left_imag, right_real, right_imag):
    real_part = matmul_high(left_real, right_real) - matmul_high(left_imag, right_imag)
    imag_part = matmul_high(left_real, right_imag) + matmul_high(left_imag, right_real)
    return (real_part, imag_part)


def panel_columns(flat_panels):
    stack_depth = flat_panels.shape[0]
    row_count = flat_panels.shape[2]
    panel_width = flat_panels.shape[3]
    upper_rows = jnp.concatenate([flat_panels[:, 0], flat_panels[:, 1]], axis=-1)
    lower_rows = jnp.concatenate([-flat_panels[:, 1], flat_panels[:, 0]], axis=-1)
    upper_rows = jnp.moveaxis(upper_rows, 0, 1).reshape(row_count, stack_depth * 2 * panel_width)
    lower_rows = jnp.moveaxis(lower_rows, 0, 1).reshape(row_count, stack_depth * 2 * panel_width)
    return (upper_rows, lower_rows)


def column_product(stored_columns, upper_rows, lower_rows):
    contract_dims = (((0,), (0,)), ((), ()))
    first_term = lax.dot_general(
        stored_columns[0], upper_rows, contract_dims, preferred_element_type=jnp.float32
    )
    second_term = lax.dot_general(
        stored_columns[1], lower_rows, contract_dims, preferred_element_type=jnp.float32
    )
    return first_term + second_term


def step_chain(level, base_total, parent, x_real, x_imag, panel_width):
    base_real = base_total[:, :panel_width]
    base_imag = base_total[:, panel_width:]
    if level == 0:
        return (-base_real, -base_imag)
    carry_real, carry_imag = complex_dot(x_real, x_imag, parent[level - 1, 0], parent[level - 1, 1])
    return (-(base_real + carry_real), -(base_imag + carry_imag))


def local_products(masked, level, x_real, x_imag):
    own_real = masked[level, 0].astype(jnp.float32)
    own_imag = masked[level, 1].astype(jnp.float32)
    return jnp.stack(complex_dot(own_real.T, own_imag.T, x_real, x_imag))


def step_diag(level, levels, own_total, follow_total, diag_real, diag_imag, parent, z_real, z_imag):
    y_real = diag_real - own_total[0]
    y_imag = diag_imag - own_total[1]
    if level > 0:
        back_real, back_imag = complex_dot(
            parent[level - 1, 0].T, parent[level - 1, 1].T, z_real, z_imag
        )
        y_real = y_real - back_real
        y_imag = y_imag - back_imag
    if level + 1 < levels:
        mix_real, mix_imag = complex_dot(y_real, y_imag, parent[level, 0], parent[level, 1])
        z_real = -(follow_total[0].T + mix_real)
        z_imag = -(follow_total[1].T + mix_imag)
    return (y_real, y_imag, z_real, z_imag)


def per_device(inverse_block, panels, panel_mask, parent_panels, diag_inverse, pole_weights):
    levels = panels.shape[1]
    block_rows = panels.shape[5]
    panel_width = panels.shape[6]
    blocks = inverse_block[0, :, :, 0]
    local_rows = blocks.shape[3]
    block_flags = panel_mask[:, 0, 0].astype(jnp.bfloat16)
    masked = panels[0, :, :, 0, 0] * block_flags[:, None, None, None]
    shard_piece = gather_axes(masked[:, :, None], COL, 2)
    stack_depth = shard_piece.shape[0]
    pieces = shard_piece.shape[2]
    columns = blocks.reshape(2, pieces * block_rows, local_rows)
    upper_rows, lower_rows = panel_columns(
        shard_piece.reshape(stack_depth, 2, pieces * block_rows, panel_width)
    )
    partial_value = column_product(columns, upper_rows, lower_rows)
    summed = summed_on_arrival(partial_value, "row", 0)
    row_totals = [
        summed[:, level * 2 * panel_width : (level + 1) * 2 * panel_width]
        for level in range(levels)
    ]
    parent = parent_panels[0]
    diag_blocks = diag_inverse[0]
    weight_real = pole_weights[0, 0]
    weight_imag = pole_weights[0, 1]
    panel_terms = []
    diag_terms = []
    density_diag = None
    x_real = None
    x_imag = None
    z_real = None
    z_imag = None
    leader = ((lax.axis_index("row") == 0) & (lax.axis_index(COL) == 0)).astype(jnp.float32)
    for level in range(levels):
        x_real, x_imag = step_chain(level, row_totals[level], parent, x_real, x_imag, panel_width)
        own_local = local_products(masked, level, x_real, x_imag)
        follow_local = (
            local_products(masked, level + 1, x_real, x_imag) if level + 1 < levels else None
        )
        y_real, y_imag, z_real, z_imag = step_diag(
            level,
            levels,
            own_local,
            follow_local,
            leader * diag_blocks[level, 0],
            leader * diag_blocks[level, 1],
            parent,
            z_real,
            z_imag,
        )
        panel_terms.append(weight_real * x_imag + weight_imag * x_real)
        diag_terms.append(weight_real * y_imag + weight_imag * y_real)
    density_diag = lax.psum(jnp.stack(diag_terms), POLE_ROW_COL)
    panel_parts = [summed_on_arrival(panel_term, "pole", 1) for panel_term in panel_terms]
    density_panel = jnp.stack(panel_parts)
    return (density_panel[:, None, None], density_diag)


def solution(mesh):
    torus = Mesh(
        mesh.devices.reshape(mesh.shape["pole"], mesh.shape["row"], 8, 2),
        ("pole", "row", "col_0", "col_1"),
    )
    placed = (
        P("pole", None, None, "row", None, COL),
        P("pole", None, None, COL, "row", None, None),
        P(None, COL, "row"),
        P("pole", None, None, None, None),
        P("pole", None, None, None, None),
        P("pole", None),
    )
    return jax.shard_map(
        per_device,
        mesh=torus,
        in_specs=placed,
        out_specs=(P(None, COL, "row", None, "pole"), P()),
        check_vma=False,
    )
```

profile of v0, /device:TPU:1, one launch (start us, length us, event | category | flops | bytes accessed | tf_op | source)
XLA Modules:
  0.0 434.6 jit_solution(2022024072475409172)
XLA Ops:
  7.9 1.0 bitcast_multiply_fusion.1
  8.9 15.0 %all_gather.6 = bf16[3,2,2,64,256]{4,3,2,1,0:T(8,128)(2,1)} all-gather(bf16[3,2,1,64,256]{4,3,2,1,0:T(8,128)(2,1)S(1)} %bitcast_multiply_fusion.1), channel_id=1, replica_groups=mesh['pole'=8,'row'=4,'col_0'=8,'col_1'=2] {'col_1'}, dimensions={2}, use_global_device_ids=true | all-gather | bytes 589824 | tf_op jit(solution)/shard_map/all_gather | solution.py:14
  23.9 2.3 fusion.63
  26.2 50.4 %all-gather.2.cloned.1.call-done = bf16[3,2,16,64,256]{4,3,2,1,0:T(8,128)(2,1)} async-done(((bf16[3,2,2,64,256]{4,3,2,1,0:T(8,128)(2,1)}), bf16[3,2,16,64,256]{4,3,2,1,0:T(8,128)(2,1)}) %all-gather.2.cloned.1.call-update) | async-done | bytes 3145744 | tf_op jit(solution)/shard_map/all_gather | solution.py:14
  76.6 2.2 slice_bitcast_fusion.1
  79.5 2.0 maximum_bitcast_fusion.1
  81.5 4.7 %copy.18 = bf16[1024,3,512]{0,2,1:T(8,128)(2,1)} copy(bf16[1024,3,512]{2,0,1:T(8,128)(2,1)} %get-tuple-element.5) | data formatting | bytes 6291456 | tf_op jit(solution)/shard_map/transpose | solution.py:48
  86.2 3.1 copy.19
  89.3 3.2 fusion.65
  92.5 2.2 convolution_add_fusion
  94.7 4.1 all-to-all-start
  99.5 18.1 %all-to-all-done = f32[4,64,1536]{2,1,0:T(8,128)S(1)} async-done(((f32[4,64,1536]{2,1,0:T(8,128)}), f32[4,64,1536]{2,1,0:T(8,128)S(1)}, u32[]{:S(2)}, u32[]{:S(2)}) %all-to-all-start) | async-done | bytes 1572896 | tf_op jit(solution)/shard_map/all_to_all | solution.py:26
  119.3 1.3 fusion.24
  122.2 1.6 multiply_add_fusion.1
  130.9 2.1 add_bitcast_fusion
  133.6 2.2 multiply_add_fusion
  138.8 0.8 fusion.50
  139.7 0.9 copy.22
  141.3 7.8 %all-to-all-start.3 = ((f32[8,1,2048]{2,1,0:T(1,128)}), f32[8,1,2048]{2,1,0:T(1,128)S(1)}, u32[]{:S(2)}, u32[]{:S(2)}) async-start(f32[8,1,2048]{2,1,0:T(1,128)} %reshape.64), calls=%async_computation.3 | async-start | bytes 131072 | tf_op jit(solution)/shard_map/all_to_all | solution.py:26
  149.2 1.3 fusion.19
  150.5 1.3 fusion.18
  151.8 1.9 pad_maximum_fusion
  154.5 5.1 %all-to-all-start.2 = ((f32[8,1,2048]{2,1,0:T(1,128)}), f32[8,1,2048]{2,1,0:T(1,128)S(1)}, u32[]{:S(2)}, u32[]{:S(2)}) async-start(f32[8,1,2048]{2,1,0:T(1,128)} %reshape.66), calls=%async_computation.2 | async-start | bytes 131072 | tf_op jit(solution)/shard_map/all_to_all | solution.py:26
  159.6 1.3 multiply_add_fusion.2
  162.4 0.8 reduce
  163.3 1.4 all-to-all-done.2
  164.7 4.1 all-to-all-start.1
  168.8 0.8 reduce.1
  169.7 4.2 all-to-all-done.1
  173.9 0.8 reduce.2
  175.5 250.3 %all-reduce.2.cloned.1.call-done = f32[3,256,256]{2,1,0:T(8,128)} async-done(((f32[3,256,256]{2,1,0:T(8,128)}), f32[3,256,256]{2,1,0:T(8,128)}) %all-reduce.2.cloned.1.call-update) | async-done | bytes 786448 | tf_op jit(solution)/shard_map/psum | solution.py:147
  425.7 2.1 copy.41
  (75 shorter events, 19.7 us)
Async XLA Ops:
  7.2 69.4 %all-gather.2.cloned.1.call-start = ((), (), s32[]{:S(2)}) async-start(), calls=%async_computation.4 | async-start | bytes 3538944 | tf_op jit(solution)/shard_map/all_gather | solution.py:14
  76.6 2.8 copy-start.2
  89.3 3.2 copy-start.1
  89.3 3.2 copy-start.3
  94.7 4.1 copy-start.6
  94.7 4.8 %copy-start.5 = (bf16[1,3,2,1,1,64,256]{6,5,4,3,2,1,0:T(8,128)(2,1)S(1)}, bf16[1,3,2,1,1,64,256]{6,5,4,3,2,1,0:T(8,128)(2,1)}, u32[]{:S(2)}) copy-start(bf16[1,3,2,1,1,64,256]{6,5,4,3,2,1,0:T(8,128)(2,1)} %param.7) | copy-start | bytes 589828
  94.7 23.1 %copy-start = (f32[1,2,2,256,256]{4,3,2,1,0:T(8,128)S(1)}, f32[1,2,2,256,256]{4,3,2,1,0:T(8,128)}, u32[]{:S(2)}) copy-start(f32[1,2,2,256,256]{4,3,2,1,0:T(8,128)} %param.9) | copy-start | bytes 3145732
  94.7 23.0 %all-to-all-start = ((f32[4,64,1536]{2,1,0:T(8,128)}), f32[4,64,1536]{2,1,0:T(8,128)S(1)}, u32[]{:S(2)}, u32[]{:S(2)}) async-start(f32[4,64,1536]{2,1,0:T(8,128)} %bitcast.238), calls=%async_computation | async-start | bytes 3145728 | tf_op jit(solution)/shard_map/all_to_all | solution.py:26
  118.6 6.4 %copy-start.4 = (f32[1,3,2,256,256]{4,3,2,1,0:T(8,128)S(1)}, f32[1,3,2,256,256]{4,3,2,1,0:T(8,128)}, u32[]{:S(2)}) copy-start(f32[1,3,2,256,256]{4,3,2,1,0:T(8,128)} %param.10) | copy-start | bytes 4718596
  141.3 13.2 %all-to-all-start.3 = ((f32[8,1,2048]{2,1,0:T(1,128)}), f32[8,1,2048]{2,1,0:T(1,128)S(1)}, u32[]{:S(2)}, u32[]{:S(2)}) async-start(f32[8,1,2048]{2,1,0:T(1,128)} %reshape.64), calls=%async_computation.3 | async-start | bytes 131072 | tf_op jit(solution)/shard_map/all_to_all | solution.py:26
  149.2 276.5 %all-reduce.2.cloned.1.call-start = ((), (), s32[]{:S(2)}) async-start(), calls=%async_computation.5 | async-start | bytes 1572864 | tf_op jit(solution)/shard_map/psum | solution.py:147
  154.5 10.2 %all-to-all-start.2 = ((f32[8,1,2048]{2,1,0:T(1,128)}), f32[8,1,2048]{2,1,0:T(1,128)S(1)}, u32[]{:S(2)}, u32[]{:S(2)}) async-start(f32[8,1,2048]{2,1,0:T(1,128)} %reshape.66), calls=%async_computation.2 | async-start | bytes 131072 | tf_op jit(solution)/shard_map/all_to_all | solution.py:26
  164.7 9.2 %all-to-all-start.1 = ((f32[8,1,2048]{2,1,0:T(1,128)}), f32[8,1,2048]{2,1,0:T(1,128)S(1)}, u32[]{:S(2)}, u32[]{:S(2)}) async-start(f32[8,1,2048]{2,1,0:T(1,128)} %reshape.68), calls=%async_computation.1 | async-start | bytes 131072 | tf_op jit(solution)/shard_map/all_to_all | solution.py:26
Sparse Core Ops, SparseCore 0:
  24.0 52.5 all-gather.1
  155.6 270.1 all-reduce.1
where the time goes:
time: 436 us; the launch traced here: 435 us
  waiting for transfers between devices  324 us (74%)
  matrix products  27.3 us (6%)
  starting transfers between devices  21.2 us (5%)
  local copies, waits for them, and re-layouts  19.8 us (5%)
  blocking collectives  15 us (3%)
  between operations  14.5 us (3%)
  other arithmetic  12.3 us (3%)
    psum x1, waiting for transfers between devices, per_device(): density_diag = lax.psum(jnp.stack(diag_terms), POLE_ROW_COL)  250 us
    all_gather x1, waiting for transfers between devices, gather_axes(): whole = lax.all_gather(whole, axes[number], axis=dim, tiled=True)  50.4 us
    all_to_all x4, waiting for transfers between devices, summed_on_arrival(): lax.all_to_all(in_blocks(array, dim, devices), axis, 0, 0, tiled=True)  23.8 us
    dot_general x44, matrix products, matmul_high(): jnp.dot(left_side, right_side, precision=lax.Precision.HIGHEST, preferred...  21.9 us
    all_to_all x4, starting transfers between devices, summed_on_arrival(): lax.all_to_all(in_blocks(array, dim, devices), axis, 0, 0, tiled=True)  21.2 us
    all_gather x1, blocking collectives, gather_axes(): whole = lax.all_gather(whole, axes[number], axis=dim, tiled=True)  15 us
  transfers between devices with their start and end apart: 6, of which 5 were waited for; matrix products, arithmetic and copies ran while one was open for 3% of the time, Pallas kernels for 0%

commit v1 on v0

v1 whole, which is shorter than its diff:
```python
import jax
import jax.numpy as jnp
from jax import lax
from jax.experimental import pallas as pl
from jax.experimental.pallas import tpu as pltpu
from jax.sharding import Mesh
from jax.sharding import PartitionSpec as P

F32 = jnp.float32
BF16 = jnp.bfloat16
MESH = pl.DeviceIdType.MESH
POLE = ("zl", "core")
COL = ("y", "zh")
NZL, NC, NX, NY, NZH = 4, 2, 4, 8, 2
NZ = NZL * NZH
NQ = NX * NC
NP = NZL * NC
NA = NY * NZH


def split(value):
    high = value.astype(BF16)
    low = (value - high.astype(F32)).astype(BF16)
    return high, low


def dot(left, right):
    return lax.dot_general(left, right, (((1,), (0,)), ((), ())), preferred_element_type=F32)


def dot_exact_left(left, right_high, right_low):
    return dot(left, right_high) + dot(left, right_low)


def dot_split(left, right):
    return dot(left[0], right[0]) + (dot(left[1], right[0]) + dot(left[0], right[1]))


def turned(real, imag):
    upper = jnp.concatenate([real, imag], axis=1)
    lower = jnp.concatenate([imag, -real], axis=1)
    return jnp.concatenate([upper, lower], axis=0)


def kernel(
    inv_ref, pan_ref, mask_ref, par_ref, dia_ref, weight_ref,
    panel_out, diag_out,
    g_in, g_t, par_v, dia_v, gath, near, p_t, q_big, q_t, sent, got,
    pole_sent, pole_got, z_sent, z_got, y_got, z_all, whole,
    load_sem, y_send, y_recv, zh_send, x_send, x_recv, ab_send, ab_recv,
    p_send, p_recv, zr_send, zr_recv, yg_send, yg_recv, zg_send, zg_recv,
    fx_send, fc_send, f_recv,
):
    zl = lax.axis_index("zl")
    core = lax.axis_index("core")
    x = lax.axis_index("x")
    y = lax.axis_index("y")
    zh = lax.axis_index("zh")
    z = zh * NZL + zl
    q = x * NC + core
    pole = zl * NC + core
    own = y * NZH + zh
    other = y * NZH + (1 - zh)

    def remote(source, target, send, recv, **where):
        return pltpu.make_async_remote_copy(
            src_ref=source, dst_ref=target, send_sem=send, recv_sem=recv,
            device_id=where, device_id_type=MESH,
        )

    def each(count, body):
        def step(index, carry):
            body(index)
            return carry
        lax.fori_loop(0, count, step, 0)

    loads = [
        pltpu.make_async_copy(inv_ref, g_in, load_sem.at[0]),
        pltpu.make_async_copy(par_ref, par_v, load_sem.at[1]),
        pltpu.make_async_copy(dia_ref, dia_v, load_sem.at[2]),
    ]
    for load in loads:
        load.start()

    barrier = pltpu.get_barrier_semaphore()

    def greet(**where):
        pl.semaphore_signal(barrier, inc=1, device_id=where, device_id_type=MESH)

    each(NY - 1, lambda i: greet(y=lax.rem(y + 1 + i, NY)))

    def greet_z(i):
        to = lax.rem(z + 1 + i, NZ)
        greet(zl=lax.rem(to, NZL), zh=to // NZL)

    each(NZ - 1, greet_z)

    def greet_q(i):
        to = lax.rem(q + 1 + i, NQ)
        greet(x=to // NC, core=lax.rem(to, NC))

    each(NQ - 1, greet_q)
    each(NZL - 1, lambda i: greet(zl=lax.rem(zl + 1 + i, NZL), core=1 - core))

    for level in range(3):
        flag = mask_ref[level].astype(F32)
        for part in range(2):
            block = (pan_ref[level, part].astype(F32) * flag).astype(BF16)
            gath[level, own, part] = block
            near[level, x, part] = block

    pl.semaphore_wait(barrier, NY - 1 + NZ - 1 + NQ - 1 + NZL - 1)

    def send_zh(level):
        return remote(
            gath.at[level, own], gath.at[level, own], zh_send.at[level], y_recv.at[level, own], zh=1 - zh
        )

    def send_y(level, part, block, i):
        offset = 4 + ((i + 1) // 2) * (1 - 2 * lax.rem(i, 2))
        return remote(
            gath.at[level, block], gath.at[level, block],
            y_send.at[level, part, i], y_recv.at[level, block], y=lax.rem(y + offset, NY),
        )

    def send_x(level, i):
        return remote(
            near.at[level, x], near.at[level, x], x_send.at[level, i], x_recv.at[level, x],
            x=lax.rem(x + 1 + i, NX),
        )

    for level in range(3):
        send_zh(level).start()
    for level in range(3):
        each(NY - 1, lambda i, level=level: send_y(level, 0, own, i).start())
        each(NX - 1, lambda i, level=level: send_x(level, i).start())
        remote(
            gath.at[level, other], gath.at[level, other], zh_send.at[level], y_recv.at[level, other], zh=1 - zh
        ).wait_recv()
        each(NY - 1, lambda i, level=level: send_y(level, 1, other, i).start())

    for load in loads:
        load.wait()
    weight_real = weight_ref[0]
    weight_imag = weight_ref[1]
    for part in range(2):
        g_t[:, part * 1024 : (part + 1) * 1024] = g_in[part].reshape(1024, 256).T
    for step in range(2):
        real = split(par_v[step, 0])
        imag = split(par_v[step, 1])
        for piece in range(2):
            q_big[step, piece, :256, :256] = real[piece]
            q_big[step, piece, :256, 256:] = imag[piece]
            q_big[step, piece, 256:, :256] = -imag[piece]
            q_big[step, piece, 256:, 256:] = real[piece]
            q_t[step, piece, :, :256] = real[piece].T
            q_t[step, piece, :, 256:] = -imag[piece].T
    first = (x == 0) & (y == 0) & (zh == 0)
    leader = jnp.where(first, 1.0, 0.0).astype(F32)

    def wait_x(level, i):
        source = lax.rem(x + 1 + i, NX)
        remote(
            near.at[level, source], near.at[level, source], x_send.at[level, i], x_recv.at[level, source], x=source
        ).wait_recv()

    def wait_y(level, i):
        source = lax.rem(y + 1 + i, NY)
        for half in range(NZH):
            block = source * NZH + half
            remote(
                gath.at[level, block], gath.at[level, block], y_send.at[level, 0, i],
                y_recv.at[level, block], y=source,
            ).wait_recv()

    for level in range(3):
        each(NX - 1, lambda i, level=level: wait_x(level, i))
        p_t[level, :, :256] = near[level, :, 0].reshape(256, 256).T
        p_t[level, :, 256:] = -(near[level, :, 1].reshape(256, 256).T)

    carry = None
    back = None
    for level in range(3):
        each(NY - 1, lambda i, level=level: wait_y(level, i))
        p_real = gath[level, :, 0].reshape(1024, 256)
        p_imag = gath[level, :, 1].reshape(1024, 256)
        g_real = g_t[:, :1024]
        g_imag = g_t[:, 1024:]
        b_real = dot(g_real, p_real) - dot(g_imag, p_imag)
        b_imag = dot(g_real, p_imag) + dot(g_imag, p_real)
        x_real = -(weight_real * b_real - weight_imag * b_imag)
        x_imag = -(weight_real * b_imag + weight_imag * b_real)
        if level > 0:
            x_real = x_real - carry[:, :256]
            x_imag = x_imag - carry[:, 256:]
        d_real = leader * (weight_real * dia_v[level, 0] - weight_imag * dia_v[level, 1])
        d_imag = leader * (weight_real * dia_v[level, 1] + weight_imag * dia_v[level, 0])
        if level < 2:
            x_high, x_low = split(jnp.concatenate([x_real, x_imag], axis=1))
            round_high, round_low = split(turned(x_real, x_imag))
            w_both = dot_exact_left(p_t[level], round_high, round_low)
            y_real = d_real - w_both[:, :256]
            y_imag = d_imag - w_both[:, 256:]
            if level > 0:
                y_real = y_real - back[:, :256]
                y_imag = y_imag - back[:, 256:]
        else:
            columns = jnp.concatenate([x_imag, -x_real], axis=0)
            col_high, col_low = split(columns)
            y_imag = d_imag - dot_exact_left(p_t[level], col_high, col_low) - back[:, 256:]
        for to in range(NQ):
            sent[level, to, :32] = x_imag[32 * to : 32 * to + 32]
            sent[level, to, 32:] = y_imag[32 * to : 32 * to + 32]

        def send_q(i, level=level):
            to = lax.rem(q + 1 + i, NQ)
            remote(
                sent.at[level, to], got.at[level, q], ab_send.at[level, i], ab_recv.at[level, q],
                x=to // NC, core=lax.rem(to, NC),
            ).start()

        each(NQ - 1, send_q)
        if level < 2:
            q_pieces = (q_big[level, 0], q_big[level, 1])
            carry = dot_split((x_high, x_low), q_pieces)
            follow = dot_exact_left(p_t[level + 1], round_high, round_low)
            mix = dot_split(split(jnp.concatenate([y_real, y_imag], axis=1)), q_pieces)
            z_real = -(follow[:, :256].T + mix[:, :256])
            z_imag = -(follow[:, 256:].T + mix[:, 256:])
            back = dot_split((q_t[level, 0], q_t[level, 1]), split(turned(z_real, z_imag)))

    def wait_q(level, i):
        source = lax.rem(q + 1 + i, NQ)
        remote(
            sent.at[level, 0], got.at[level, source], ab_send.at[level, i], ab_recv.at[level, source],
            x=source // NC, core=lax.rem(source, NC),
        ).wait_recv()

    panel_sums = []
    for level in range(3):
        each(NQ - 1, lambda i, level=level: wait_q(level, i))
        got[level, q] = sent[level, q]
        total = got[level, 0]
        for source in range(1, NQ):
            total = total + got[level, source]
        panel_sums.append(total[:32])
        for tile in range(NZ):
            row, column = 8 * (tile // 2), 128 * (tile % 2)
            z_sent[tile, level] = total[32 + row : 40 + row, column : column + 128]

    def send_zr(i):
        to = lax.rem(z + 1 + i, NZ)
        return remote(
            z_sent.at[to], z_got.at[z], zr_send.at[i], zr_recv.at[z], zl=lax.rem(to, NZL), zh=to // NZL
        )

    each(NZ - 1, lambda i: send_zr(i).start())
    panel_sums.append(jnp.zeros((32, 256), F32))
    pole_sent[...] = jnp.concatenate(panel_sums, axis=0).T.reshape(NP, 32, 128)

    def send_p(i):
        to = lax.rem(pole + 1 + i, NP)
        return remote(
            pole_sent.at[to], pole_got.at[pole], p_send.at[i], p_recv.at[pole],
            zl=to // NC, core=lax.rem(to, NC),
        )

    each(NP - 1, lambda i: send_p(i).start())

    def wait_zr(i):
        source = lax.rem(z + 1 + i, NZ)
        remote(
            z_sent.at[0], z_got.at[source], zr_send.at[i], zr_recv.at[source],
            zl=lax.rem(source, NZL), zh=source // NZL,
        ).wait_recv()

    each(NZ - 1, wait_zr)
    z_got[z] = z_sent[z]
    total = z_got[0]
    for source in range(1, NZ):
        total = total + z_got[source]
    y_got[y] = total

    def send_yg(i):
        return remote(
            y_got.at[y], y_got.at[y], yg_send.at[i], yg_recv.at[y], y=lax.rem(y + 1 + i, NY)
        )

    each(NY - 1, lambda i: send_yg(i).start())

    def wait_p(i):
        source = lax.rem(pole + 1 + i, NP)
        remote(
            pole_sent.at[0], pole_got.at[source], p_send.at[i], p_recv.at[source],
            zl=source // NC, core=lax.rem(source, NC),
        ).wait_recv()

    each(NP - 1, wait_p)
    pole_got[pole] = pole_sent[pole]
    for half in range(NC):
        total = pole_got[half]
        for layer in range(1, NZL):
            total = total + pole_got[layer * NC + half]
        rows = total.T
        for level in range(3):
            panel_out[level, 32 * half : 32 * half + 32] = rows[32 * level : 32 * level + 32]

    def wait_yg(i):
        source = lax.rem(y + 1 + i, NY)
        remote(
            y_got.at[source], y_got.at[source], yg_send.at[i], yg_recv.at[source], y=source
        ).wait_recv()

    each(NY - 1, wait_yg)
    total = y_got[0]
    for source in range(1, NY):
        total = total + y_got[source]
    whole[q, z] = total

    def send_zg(i):
        to = lax.rem(z + 1 + i, NZ)
        return remote(
            whole.at[q, z], whole.at[q, z], zg_send.at[i], zg_recv.at[z], zl=lax.rem(to, NZL), zh=to // NZL
        )

    each(NZ - 1, lambda i: send_zg(i).start())

    def wait_zg(i):
        source = lax.rem(z + 1 + i, NZ)
        remote(
            whole.at[q, source], whole.at[q, source], zg_send.at[i], zg_recv.at[source],
            zl=lax.rem(source, NZL), zh=source // NZL,
        ).wait_recv()

    each(NZ - 1, wait_zg)

    def send_fx(i):
        return remote(
            whole.at[q], whole.at[q], fx_send.at[i], f_recv.at[q], x=lax.rem(x + 1 + i, NX)
        )

    def send_fc(i):
        block = lax.rem(x + i, NX) * NC + core
        return remote(
            whole.at[block], whole.at[block], fc_send.at[i], f_recv.at[block], core=1 - core
        )

    def wait_f(block, i):
        remote(
            whole.at[block], whole.at[block], fc_send.at[i], f_recv.at[block], core=1 - core
        ).wait_recv()

    each(NX - 1, lambda i: send_fx(i).start())
    send_fc(0).start()

    def relay(i):
        wait_f(lax.rem(x + 1 + i, NX) * NC + core, 1 + i)
        send_fc(1 + i).start()

    each(NX - 1, relay)
    each(NX, lambda i: wait_f(lax.rem(x + i, NX) * NC + (1 - core), i))
    for source in range(NQ):
        for tile in range(NZ):
            row, column = 32 * source + 8 * (tile // 2), 128 * (tile % 2)
            diag_out[:, row : row + 8, column : column + 128] = whole[source, tile]

    for level in range(3):
        send_zh(level).wait_send()

        def drain(i, level=level):
            send_y(level, 0, own, i).wait_send()
            send_y(level, 1, other, i).wait_send()
            to = lax.rem(q + 1 + i, NQ)
            remote(
                sent.at[level, to], got.at[level, q], ab_send.at[level, i], ab_recv.at[level, q],
                x=to // NC, core=lax.rem(to, NC),
            ).wait_send()

        each(NY - 1, drain)
        each(NX - 1, lambda i, level=level: send_x(level, i).wait_send())

    def drain_tail(i):
        send_zr(i).wait_send()
        send_p(i).wait_send()
        send_yg(i).wait_send()
        send_zg(i).wait_send()

    each(NZ - 1, drain_tail)
    each(NX - 1, lambda i: send_fx(i).wait_send())
    each(NX, lambda i: send_fc(i).wait_send())


def per_device(inverse_block, panels, panel_mask, parent_panels, diag_inverse, pole_weights):
    any_space = pl.BlockSpec(memory_space=pl.ANY)
    vmem = pl.BlockSpec(memory_space=pltpu.VMEM)
    smem = pl.BlockSpec(memory_space=pltpu.SMEM)
    dma = pltpu.SemaphoreType.DMA
    panel, diag = pl.pallas_call(
        kernel,
        out_shape=(
            jax.ShapeDtypeStruct((3, 64, 32), F32),
            jax.ShapeDtypeStruct((3, 256, 256), F32),
        ),
        in_specs=[any_space, vmem, smem, any_space, any_space, smem],
        out_specs=(vmem, vmem),
        scratch_shapes=[
            pltpu.VMEM((2, NA, 64, 256), BF16),
            pltpu.VMEM((256, 2048), BF16),
            pltpu.VMEM((2, 2, 256, 256), F32),
            pltpu.VMEM((3, 2, 256, 256), F32),
            pltpu.VMEM((3, NA, 2, 64, 256), BF16),
            pltpu.VMEM((3, NX, 2, 64, 256), BF16),
            pltpu.VMEM((3, 256, 512), BF16),
            pltpu.VMEM((2, 2, 512, 512), BF16),
            pltpu.VMEM((2, 2, 256, 512), BF16),
            pltpu.VMEM((3, NQ, 64, 256), F32),
            pltpu.VMEM((3, NQ, 64, 256), F32),
            pltpu.VMEM((NP, 32, 128), F32),
            pltpu.VMEM((NP, 32, 128), F32),
            pltpu.VMEM((NZ, 3, 8, 128), F32),
            pltpu.VMEM((NZ, 3, 8, 128), F32),
            pltpu.VMEM((NY, 3, 8, 128), F32),
            pltpu.VMEM((NZ, 3, 8, 128), F32),
            pltpu.VMEM((NQ, NZ, 3, 8, 128), F32),
            dma((3,)), dma((3, 2, NY)), dma((3, NA)), dma((3,)), dma((3, NX)), dma((3, NX)),
            dma((3, NQ)), dma((3, NQ)), dma((NP,)), dma((NP,)), dma((NZ,)), dma((NZ,)),
            dma((NY,)), dma((NY,)), dma((NZ,)), dma((NZ,)), dma((NX,)), dma((NX,)), dma((NQ,)),
        ],
        compiler_params=pltpu.CompilerParams(collective_id=0, has_side_effects=True),
    )(
        inverse_block[0, :, :, 0],
        panels[0, :, :, 0, 0],
        panel_mask[:, 0, 0],
        parent_panels[0],
        diag_inverse[0],
        pole_weights[0],
    )
    return panel[:, None, None], diag


def solution(mesh):
    torus = Mesh(
        mesh.devices.reshape(NZL, NC, NX, NY, NZH), ("zl", "core", "x", "y", "zh")
    )
    placed = (
        P(POLE, None, None, "x", None, COL),
        P(POLE, None, None, COL, "x", None, None),
        P(None, COL, "x"),
        P(POLE, None, None, None, None),
        P(POLE, None, None, None, None),
        P(POLE, None),
    )
    return jax.shard_map(
        per_device,
        mesh=torus,
        in_specs=placed,
        out_specs=(P(None, COL, "x", None, POLE), P()),
        check_vma=False,
    )
```

time: 436 us -> 125 us (0.29)
  waiting for transfers between devices: 324 us -> 0 us
  Pallas kernels: 0 us -> 120 us
  matrix products: 27.3 us -> 0 us
  starting transfers between devices: 21.2 us -> 0 us
  local copies, waits for them, and re-layouts: 19.8 us -> 3.67 us
  blocking collectives: 15 us -> 0 us
  between operations: 14.5 us -> 0.64 us
  other arithmetic: 12.3 us -> 0 us
    psum x1 -> x0, waiting for transfers between devices: 250 us -> none  [per_device(): density_diag = lax.psum(jnp.stack(diag_terms), POLE_ROW_COL)]
    pallas_call x0 -> x1, Pallas kernels: none -> 120 us  [per_device(): pl.pallas_call(kernel, out_shape=(jax.ShapeDtypeStruct((3, 64, 32), F32),...]
    all_gather x1 -> x0, waiting for transfers between devices: 50.4 us -> none  [gather_axes(): whole = lax.all_gather(whole, axes[number], axis=dim, tiled=True)]
    dot_general x46 -> x0, matrix products: 27.3 us -> none  [the longest x44 21.9 us: matmul_high(): jnp.dot(left_side, right_side, precision=lax.Precision.HIGHEST, preferred...]
    all_to_all x4 -> x0, waiting for transfers between devices: 23.8 us -> none  [summed_on_arrival(): lax.all_to_all(in_blocks(array, dim, devices), axis, 0, 0, tiled=True)]
    all_to_all x4 -> x0, starting transfers between devices: 21.2 us -> none  [summed_on_arrival(): lax.all_to_all(in_blocks(array, dim, devices), axis, 0, 0, tiled=True)]
    all_gather x1 -> x0, blocking collectives: 15 us -> none  [gather_axes(): whole = lax.all_gather(whole, axes[number], axis=dim, tiled=True)]
    transpose x2 -> x0, local copies, waits for them, and re-layouts: 7.77 us -> none  [the longest x1 4.71 us: panel_columns(): jnp.moveaxis(upper_rows, 0, 1)]
  transfers between devices with their start and end apart: 6 -> 0, of which waited for: 5 -> 0; matrix products, arithmetic and copies ran while one was open for 3% -> 0% of each run, Pallas kernels for 0% -> 0%
where the time goes in v1:
time: 125 us; the launch traced here: 124 us
  Pallas kernels  120 us (96%)
  local copies, waits for them, and re-layouts  3.67 us (3%)
    pallas_call x1, Pallas kernels, per_device(): pl.pallas_call(kernel, out_shape=(jax.ShapeDtypeStruct((3, 64, 32), F32),...  120 us
    unnamed x2, local copies, waits for them, and re-layouts  3.67 us

profile of v1, /device:TPU:1, one launch (start us, length us, event | category | flops | bytes accessed | tf_op | source)
XLA Modules:
  0.0 124.4 jit_solution(1747690532352034954)
XLA Ops:
  0.6 120.1 %shard_map.77 = (f32[3,64,32]{2,1,0:T(8,128)}, f32[3,256,256]{2,1,0:T(8,128)}) custom-call(bf16[2,16,64,256]{3,2,1,0:T(8,128)(2,1)} %bitcast.8, bf16[3,2,64,256]{3,2,1,0:T(8,128)(2,1)} %bitcast.10, s32[3]{0:T(128)} %bitcast.12, f32[2,2,256,256]{3,2,1,0:T(8,128)} %bitcast.9, f32[3,2,256,256]{3,2,1,0:T(8,128)} %bitcast.7, f32[2]{0:T(128)} %bitcast.13), custom_call_target="tpu_custom_call" | custom-call | tf_op jit(solution)/shard_map/pallas_call | solution.py:398
  120.7 1.6 %copy.8 = f32[3,1,1,64,32]{3,4,2,1,0:T(8,128)} copy(f32[3,1,1,64,32]{4,3,0,2,1:T(8,128)} %bitcast.11) | data formatting | bytes 49152
  122.3 2.1 %copy.10 = f32[3,256,256]{2,1,0:T(8,128)} copy(f32[3,256,256]{2,1,0:T(8,128)} %get-tuple-element.11) | data formatting | bytes 1572864

commit v2 on v1

v2 whole, which is shorter than its diff:
```python
import jax
import jax.numpy as jnp
from jax import lax
from jax.experimental import pallas as pl
from jax.experimental.pallas import tpu as pltpu
from jax.sharding import Mesh
from jax.sharding import PartitionSpec as P

F32 = jnp.float32
BF16 = jnp.bfloat16
MESH = pl.DeviceIdType.MESH
POLE = ("zl", "core")
COL = ("y", "zh")
NZL, NC, NX, NY, NZH = 4, 2, 4, 8, 2
NZ = NZL * NZH
NQ = NX * NC
NP = NZL * NC
NA = NY * NZH
GROUPS = ((0, 1), (2,))

PLAN = (
    "o20", "p", "o21", "p", "o30", "p", "t10", "p", "o31", "p", "t20", "p", "t11", "p", "o40", "p", "t30",
    "p", "t21", "p", "t40", "p", "o22", "p", "t31", "p", "t12", "p", "o41", "t41", "c", "o32", "c", "t22",
    "c", "o42", "c", "t32", "c", "c", "t42", "c", "c",
)


def split(value):
    high = value.astype(BF16)
    low = (value - high.astype(F32)).astype(BF16)
    return high, low


def dot(left, right):
    return lax.dot_general(left, right, (((1,), (0,)), ((), ())), preferred_element_type=F32)


def dot_exact_left(left, right_high, right_low):
    return dot(left, right_high) + dot(left, right_low)


def dot_split(left, right):
    return dot(left[0], right[0]) + (dot(left[1], right[0]) + dot(left[0], right[1]))


def turned(real, imag):
    upper = jnp.concatenate([real, imag], axis=1)
    lower = jnp.concatenate([imag, -real], axis=1)
    return jnp.concatenate([upper, lower], axis=0)


def kernel(
    inv_ref, pan_ref, mask_ref, par_ref, dia_ref, weight_ref,
    panel_out, diag_out,
    g_in, g_t, par_v, dia_v, gath, near, p_t, q_big, q_t, sent, got,
    pole_sent, pole_got, z_sent_early, z_sent_late, z_got_early, z_got_late,
    y_got_early, y_got_late, whole_early, whole_late,
    load_sem, y_send, y_recv, zh_send, zh_recv, x_send, x_recv, ab_send, ab_recv,
    p_send, p_recv, zr_send, zr_recv, yg_send, yg_recv, zg_send, zg_recv,
    fx_send, fc_send, f_recv,
):
    zl = lax.axis_index("zl")
    core = lax.axis_index("core")
    x = lax.axis_index("x")
    y = lax.axis_index("y")
    zh = lax.axis_index("zh")
    z = zh * NZL + zl
    q = x * NC + core
    pole = zl * NC + core
    own = y * NZH + zh
    other = y * NZH + (1 - zh)

    def remote(source, target, send, recv, **where):
        return pltpu.make_async_remote_copy(
            src_ref=source, dst_ref=target, send_sem=send, recv_sem=recv,
            device_id=where, device_id_type=MESH,
        )

    def each(count, body):
        def step(index, carry):
            body(index)
            return carry
        lax.fori_loop(0, count, step, 0)

    z_sent = (z_sent_early, z_sent_late)
    z_got = (z_got_early, z_got_late)
    y_got = (y_got_early, y_got_late)
    whole = (whole_early, whole_late)

    loads = [
        pltpu.make_async_copy(inv_ref, g_in, load_sem.at[0]),
        pltpu.make_async_copy(par_ref, par_v, load_sem.at[1]),
        pltpu.make_async_copy(dia_ref, dia_v, load_sem.at[2]),
    ]
    for load in loads:
        load.start()

    barrier = pltpu.get_barrier_semaphore()

    def greet(**where):
        pl.semaphore_signal(barrier, inc=1, device_id=where, device_id_type=MESH)

    each(NY - 1, lambda i: greet(y=lax.rem(y + 1 + i, NY)))

    def greet_z(i):
        to = lax.rem(z + 1 + i, NZ)
        greet(zl=lax.rem(to, NZL), zh=to // NZL)

    each(NZ - 1, greet_z)

    def greet_q(i):
        to = lax.rem(q + 1 + i, NQ)
        greet(x=to // NC, core=lax.rem(to, NC))

    each(NQ - 1, greet_q)
    each(NZL - 1, lambda i: greet(zl=lax.rem(zl + 1 + i, NZL), core=1 - core))

    for level in range(3):
        flag = mask_ref[level].astype(F32)
        for part in range(2):
            block = (pan_ref[level, part].astype(F32) * flag).astype(BF16)
            gath[level, own, part] = block
            near[level, x, part] = block

    pl.semaphore_wait(barrier, NY - 1 + NZ - 1 + NQ - 1 + NZL - 1)

    def send_zh(level):
        return remote(
            gath.at[level, own], gath.at[level, own], zh_send.at[level], zh_recv.at[level], zh=1 - zh
        )

    def wait_zh(level):
        remote(
            gath.at[level, other], gath.at[level, other], zh_send.at[level], zh_recv.at[level], zh=1 - zh
        ).wait_recv()

    def hop(level, way, half, distance, behind):
        source = lax.rem(y + (behind if way else NY - behind), NY)
        block = source * NZH + (1 - zh if half else zh)
        place = gath.at[level, block] if distance < 4 else gath.at[level, block, way]
        index = ((level * 2 + way) * 2 + half) * 4 + distance - 1
        return remote(
            place, place, y_send.at[index], y_recv.at[index], y=lax.rem(y + (NY - 1 if way else 1), NY)
        )

    def arrive(level, half, distance):
        for way in range(2):
            hop(level, way, half, distance, distance).wait_recv()

    def push(level, half, distance):
        for way in range(2):
            hop(level, way, half, distance, distance - 1).start()

    def send_x(level, i):
        return remote(
            near.at[level, x], near.at[level, x], x_send.at[level, i], x_recv.at[level, x],
            x=lax.rem(x + 1 + i, NX),
        )

    for level in range(3):
        send_zh(level).start()
        push(level, 0, 1)
    for level in range(3):
        each(NX - 1, lambda i, level=level: send_x(level, i).start())

    def send_q(level, kind, i):
        to = lax.rem(q + 1 + i, NQ)
        return remote(
            sent.at[level, to, kind], got.at[level, q, kind], ab_send.at[level, kind, i], ab_recv.at[level, kind, q],
            x=to // NC, core=lax.rem(to, NC),
        )

    weight_real = weight_ref[0]
    weight_imag = weight_ref[1]
    first = (x == 0) & (y == 0) & (zh == 0)
    leader = jnp.where(first, 1.0, 0.0).astype(F32)

    def wait_x(level, i):
        source = lax.rem(x + 1 + i, NX)
        remote(
            near.at[level, source], near.at[level, source], x_send.at[level, i], x_recv.at[level, source], x=source
        ).wait_recv()

    def prepare():
        for load in loads:
            load.wait()
        for part in range(2):
            for piece in range(4):
                g_t[:, part * 1024 + piece * 256 : part * 1024 + piece * 256 + 256] = (
                    g_in[part, 4 * piece : 4 * piece + 4].reshape(256, 256).T
                )
                if piece % 2:
                    yield
        for step in range(2):
            real = split(par_v[step, 0])
            imag = split(par_v[step, 1])
            for piece in range(2):
                q_big[step, piece, :256, :256] = real[piece]
                q_big[step, piece, :256, 256:] = imag[piece]
                q_big[step, piece, 256:, :256] = -imag[piece]
                q_big[step, piece, 256:, 256:] = real[piece]
                q_t[step, piece, :, :256] = real[piece].T
                q_t[step, piece, :, 256:] = -imag[piece].T
                yield
        for level in range(3):
            each(NX - 1, lambda i, level=level: wait_x(level, i))
            p_t[level, :, :256] = near[level, :, 0].reshape(256, 256).T
            p_t[level, :, 256:] = -(near[level, :, 1].reshape(256, 256).T)
            yield

    def chain():
        carry = None
        back = None
        for level in range(3):
            for half in range(2):
                arrive(level, half, 4)
            p_real = gath[level, :, 0].reshape(1024, 256)
            p_imag = gath[level, :, 1].reshape(1024, 256)
            g_real = g_t[:, :1024]
            g_imag = g_t[:, 1024:]
            b_real = dot(g_real, p_real) - dot(g_imag, p_imag)
            if level < 2:
                yield
            b_imag = dot(g_real, p_imag) + dot(g_imag, p_real)
            x_real = -(weight_real * b_real - weight_imag * b_imag)
            x_imag = -(weight_real * b_imag + weight_imag * b_real)
            if level > 0:
                x_real = x_real - carry[:, :256]
                x_imag = x_imag - carry[:, 256:]
            if level < 2:
                yield
            d_real = leader * (weight_real * dia_v[level, 0] - weight_imag * dia_v[level, 1])
            d_imag = leader * (weight_real * dia_v[level, 1] + weight_imag * dia_v[level, 0])
            if level < 2:
                x_high, x_low = split(jnp.concatenate([x_real, x_imag], axis=1))
                round_high, round_low = split(turned(x_real, x_imag))
                w_both = dot_exact_left(p_t[level], round_high, round_low)
                y_real = d_real - w_both[:, :256]
                y_imag = d_imag - w_both[:, 256:]
                if level > 0:
                    y_real = y_real - back[:, :256]
                    y_imag = y_imag - back[:, 256:]
            else:
                columns = jnp.concatenate([x_imag, -x_real], axis=0)
                col_high, col_low = split(columns)
                y_imag = d_imag - dot_exact_left(p_t[level], col_high, col_low) - back[:, 256:]
            for to in range(NQ):
                sent[level, to, 0] = y_imag[32 * to : 32 * to + 32]
            each(NQ - 1, lambda i, level=level: send_q(level, 0, i).start())
            for to in range(NQ):
                sent[level, to, 1] = x_imag[32 * to : 32 * to + 32]
            each(NQ - 1, lambda i, level=level: send_q(level, 1, i).start())
            if level < 2:
                yield
                q_pieces = (q_big[level, 0], q_big[level, 1])
                carry = dot_split((x_high, x_low), q_pieces)
                yield
                follow = dot_exact_left(p_t[level + 1], round_high, round_low)
                mix = dot_split(split(jnp.concatenate([y_real, y_imag], axis=1)), q_pieces)
                z_real = -(follow[:, :256].T + mix[:, :256])
                z_imag = -(follow[:, 256:].T + mix[:, 256:])
                yield
                back = dot_split((q_t[level, 0], q_t[level, 1]), split(turned(z_real, z_imag)))
                yield

    ready = prepare()
    work = chain()
    for step in PLAN:
        if step == "p":
            next(ready, None)
        elif step == "c":
            next(work, None)
        else:
            half, distance, level = "ot".index(step[0]), int(step[1]), int(step[2])
            if distance == 1:
                wait_zh(level)
            else:
                arrive(level, half, distance - 1)
            push(level, half, distance)
    for _ in ready:
        pass
    for _ in work:
        pass

    def sum_q(level, kind):
        def wait_q(i):
            source = lax.rem(q + 1 + i, NQ)
            remote(
                sent.at[level, 0, kind], got.at[level, source, kind], ab_send.at[level, kind, i],
                ab_recv.at[level, kind, source], x=source // NC, core=lax.rem(source, NC),
            ).wait_recv()

        each(NQ - 1, wait_q)
        got[level, q, kind] = sent[level, q, kind]
        total = got[level, 0, kind]
        for source in range(1, NQ):
            total = total + got[level, source, kind]
        return total

    def send_zr(group, i):
        to = lax.rem(z + 1 + i, NZ)
        return remote(
            z_sent[group].at[to], z_got[group].at[z], zr_send.at[group, i], zr_recv.at[group, z],
            zl=lax.rem(to, NZL), zh=to // NZL,
        )

    def send_yg(group, i):
        return remote(
            y_got[group].at[y], y_got[group].at[y], yg_send.at[group, i], yg_recv.at[group, y],
            y=lax.rem(y + 1 + i, NY),
        )

    def send_zg(group, i):
        to = lax.rem(z + 1 + i, NZ)
        place = whole[group].at[q, z]
        return remote(
            place, place, zg_send.at[group, i], zg_recv.at[group, z], zl=lax.rem(to, NZL), zh=to // NZL
        )

    def send_fx(group, i):
        place = whole[group].at[q]
        return remote(place, place, fx_send.at[group, i], f_recv.at[group, q], x=lax.rem(x + 1 + i, NX))

    def send_fc(group, i):
        block = lax.rem(x + i, NX) * NC + core
        place = whole[group].at[block]
        return remote(place, place, fc_send.at[group, i], f_recv.at[group, block], core=1 - core)

    def wait_f(group, block, i):
        place = whole[group].at[block]
        remote(place, place, fc_send.at[group, i], f_recv.at[group, block], core=1 - core).wait_recv()

    def across_z(group):
        for place, level in enumerate(GROUPS[group]):
            total = sum_q(level, 0)
            for tile in range(NZ):
                row, column = 8 * (tile // 2), 128 * (tile % 2)
                z_sent[group][tile, place] = total[row : row + 8, column : column + 128]
        each(NZ - 1, lambda i: send_zr(group, i).start())

    def across_y(group):
        def wait_zr(i):
            source = lax.rem(z + 1 + i, NZ)
            remote(
                z_sent[group].at[0], z_got[group].at[source], zr_send.at[group, i], zr_recv.at[group, source],
                zl=lax.rem(source, NZL), zh=source // NZL,
            ).wait_recv()

        each(NZ - 1, wait_zr)
        z_got[group][z] = z_sent[group][z]
        total = z_got[group][0]
        for source in range(1, NZ):
            total = total + z_got[group][source]
        y_got[group][y] = total
        each(NY - 1, lambda i: send_yg(group, i).start())

    def back_z(group):
        def wait_yg(i):
            source = lax.rem(y + 1 + i, NY)
            place = y_got[group].at[source]
            remote(place, place, yg_send.at[group, i], yg_recv.at[group, source], y=source).wait_recv()

        each(NY - 1, wait_yg)
        total = y_got[group][0]
        for source in range(1, NY):
            total = total + y_got[group][source]
        whole[group][q, z] = total
        each(NZ - 1, lambda i: send_zg(group, i).start())

    def back_x(group):
        def wait_zg(i):
            source = lax.rem(z + 1 + i, NZ)
            place = whole[group].at[q, source]
            remote(
                place, place, zg_send.at[group, i], zg_recv.at[group, source],
                zl=lax.rem(source, NZL), zh=source // NZL,
            ).wait_recv()

        each(NZ - 1, wait_zg)
        each(NX - 1, lambda i: send_fx(group, i).start())
        send_fc(group, 0).start()

    def back_core(group):
        def relay(i):
            wait_f(group, lax.rem(x + 1 + i, NX) * NC + core, 1 + i)
            send_fc(group, 1 + i).start()

        each(NX - 1, relay)

    def place_diag(group):
        each(NX, lambda i: wait_f(group, lax.rem(x + i, NX) * NC + (1 - core), i))
        for place, level in enumerate(GROUPS[group]):
            for source in range(NQ):
                for tile in range(NZ):
                    row, column = 32 * source + 8 * (tile // 2), 128 * (tile % 2)
                    diag_out[level, row : row + 8, column : column + 128] = whole[group][source, tile, place]

    def send_p(i):
        to = lax.rem(pole + 1 + i, NP)
        return remote(
            pole_sent.at[to], pole_got.at[pole], p_send.at[i], p_recv.at[pole],
            zl=to // NC, core=lax.rem(to, NC),
        )

    def wait_p(i):
        source = lax.rem(pole + 1 + i, NP)
        remote(
            pole_sent.at[0], pole_got.at[source], p_send.at[i], p_recv.at[source],
            zl=source // NC, core=lax.rem(source, NC),
        ).wait_recv()

    def both(stage):
        for group in range(2):
            stage(group)

    both(across_z)
    both(across_y)
    panel_sums = [sum_q(level, 1) for level in range(3)] + [jnp.zeros((32, 256), F32)]
    pole_sent[...] = jnp.concatenate(panel_sums, axis=0).T.reshape(NP, 32, 128)
    each(NP - 1, lambda i: send_p(i).start())
    both(back_z)
    each(NP - 1, wait_p)
    pole_got[pole] = pole_sent[pole]
    for half in range(NC):
        total = pole_got[half]
        for layer in range(1, NZL):
            total = total + pole_got[layer * NC + half]
        for level in range(3):
            panel_out[level, :, 32 * half : 32 * half + 32] = total[:, 32 * level : 32 * level + 32]
    both(back_x)
    both(back_core)
    both(place_diag)

    for level in range(3):
        send_zh(level).wait_send()

        for kind in range(2):
            each(NQ - 1, lambda i, level=level, kind=kind: send_q(level, kind, i).wait_send())
        for half in range(2):
            for distance in range(1, 5):
                for way in range(2):
                    hop(level, way, half, distance, distance - 1).wait_send()
        each(NX - 1, lambda i, level=level: send_x(level, i).wait_send())

    each(NP - 1, lambda i: send_p(i).wait_send())
    for group in range(2):

        def drain(i, group=group):
            send_zr(group, i).wait_send()
            send_yg(group, i).wait_send()
            send_zg(group, i).wait_send()

        each(NZ - 1, drain)
        each(NX - 1, lambda i, group=group: send_fx(group, i).wait_send())
        each(NX, lambda i, group=group: send_fc(group, i).wait_send())


def per_device(inverse_block, panels, panel_mask, parent_panels, diag_inverse, pole_weights):
    any_space = pl.BlockSpec(memory_space=pl.ANY)
    vmem = pl.BlockSpec(memory_space=pltpu.VMEM)
    smem = pl.BlockSpec(memory_space=pltpu.SMEM)
    dma = pltpu.SemaphoreType.DMA
    panel, diag = pl.pallas_call(
        kernel,
        out_shape=(
            jax.ShapeDtypeStruct((3, 32, 64), F32),
            jax.ShapeDtypeStruct((3, 256, 256), F32),
        ),
        in_specs=[any_space, vmem, smem, any_space, any_space, smem],
        out_specs=(vmem, vmem),
        scratch_shapes=[
            pltpu.VMEM((2, NA, 64, 256), BF16),
            pltpu.VMEM((256, 2048), BF16),
            pltpu.VMEM((2, 2, 256, 256), F32),
            pltpu.VMEM((3, 2, 256, 256), F32),
            pltpu.VMEM((3, NA, 2, 64, 256), BF16),
            pltpu.VMEM((3, NX, 2, 64, 256), BF16),
            pltpu.VMEM((3, 256, 512), BF16),
            pltpu.VMEM((2, 2, 512, 512), BF16),
            pltpu.VMEM((2, 2, 256, 512), BF16),
            pltpu.VMEM((3, NQ, 2, 32, 256), F32),
            pltpu.VMEM((3, NQ, 2, 32, 256), F32),
            pltpu.VMEM((NP, 32, 128), F32),
            pltpu.VMEM((NP, 32, 128), F32),
            pltpu.VMEM((NZ, 2, 8, 128), F32),
            pltpu.VMEM((NZ, 1, 8, 128), F32),
            pltpu.VMEM((NZ, 2, 8, 128), F32),
            pltpu.VMEM((NZ, 1, 8, 128), F32),
            pltpu.VMEM((NY, 2, 8, 128), F32),
            pltpu.VMEM((NY, 1, 8, 128), F32),
            pltpu.VMEM((NQ, NZ, 2, 8, 128), F32),
            pltpu.VMEM((NQ, NZ, 1, 8, 128), F32),
            dma((3,)), dma((48,)), dma((48,)), dma((3,)), dma((3,)), dma((3, NX)), dma((3, NX)),
            dma((3, 2, NQ)), dma((3, 2, NQ)), dma((NP,)), dma((NP,)), dma((2, NZ)), dma((2, NZ)),
            dma((2, NY)), dma((2, NY)), dma((2, NZ)), dma((2, NZ)), dma((2, NX)), dma((2, NX)), dma((2, NQ)),
        ],
        compiler_params=pltpu.CompilerParams(collective_id=0, has_side_effects=True),
    )(
        inverse_block[0, :, :, 0],
        panels[0, :, :, 0, 0],
        panel_mask[:, 0, 0],
        parent_panels[0],
        diag_inverse[0],
        pole_weights[0],
    )
    return panel.swapaxes(1, 2)[:, None, None], diag


def solution(mesh):
    torus = Mesh(
        mesh.devices.reshape(NZL, NC, NX, NY, NZH), ("zl", "core", "x", "y", "zh")
    )
    placed = (
        P(POLE, None, None, "x", None, COL),
        P(POLE, None, None, COL, "x", None, None),
        P(None, COL, "x"),
        P(POLE, None, None, None, None),
        P(POLE, None, None, None, None),
        P(POLE, None),
    )
    return jax.shard_map(
        per_device,
        mesh=torus,
        in_specs=placed,
        out_specs=(P(None, COL, "x", None, POLE), P()),
        check_vma=False,
    )
```

time: 125 us -> 93.1 us (0.74)
  Pallas kernels: 120 us -> 88.8 us
    pallas_call x1, Pallas kernels: 120 us -> 88.8 us  [per_device(): pl.pallas_call(kernel, out_shape=(jax.ShapeDtypeStruct((3, 32, 64), F32),...]
where the time goes in v2:
time: 93.1 us; the launch traced here: 92.9 us
  Pallas kernels  88.8 us (95%)
  local copies, waits for them, and re-layouts  3.48 us (4%)
    pallas_call x1, Pallas kernels, per_device(): pl.pallas_call(kernel, out_shape=(jax.ShapeDtypeStruct((3, 32, 64), F32),...  88.8 us
    unnamed x2, local copies, waits for them, and re-layouts  3.48 us

profile of v2, /device:TPU:1, one launch (start us, length us, event | category | flops | bytes accessed | tf_op | source)
XLA Modules:
  0.0 92.9 jit_solution(6812923646553083858)
XLA Ops:
  0.6 88.8 %shard_map.77 = (f32[3,32,64]{2,1,0:T(8,128)}, f32[3,256,256]{2,1,0:T(8,128)}) custom-call(bf16[2,16,64,256]{3,2,1,0:T(8,128)(2,1)} %bitcast.12, bf16[3,2,64,256]{3,2,1,0:T(8,128)(2,1)} %bitcast.14, s32[3]{0:T(128)} %bitcast.16, f32[2,2,256,256]{3,2,1,0:T(8,128)} %bitcast.13, f32[3,2,256,256]{3,2,1,0:T(8,128)} %bitcast.11, f32[2]{0:T(128)} %bitcast.17), custom_call_target="tpu_custom_call" | custom-call | tf_op jit(solution)/shard_map/pallas_call | solution.py:463
  89.4 1.4 %copy.11 = f32[3,1,1,64,32]{3,4,2,1,0:T(8,128)} copy(f32[3,1,1,64,32]{3,4,2,1,0:T(8,128)} %bitcast.15) | data formatting | bytes 49152
  90.8 2.1 %copy.12 = f32[3,256,256]{2,1,0:T(8,128)} copy(f32[3,256,256]{2,1,0:T(8,128)} %get-tuple-element.11) | data formatting | bytes 1572864

commit v3 on v2

--- a/solution.py
+++ b/solution.py
@@ -19,9 +19,9 @@
 GROUPS = ((0, 1), (2,))
 
 PLAN = (
-    "o20", "p", "o21", "p", "o30", "p", "t10", "p", "o31", "p", "t20", "p", "t11", "p", "o40", "p", "t30",
-    "p", "t21", "p", "t40", "p", "o22", "p", "t31", "p", "t12", "p", "o41", "t41", "c", "o32", "c", "t22",
-    "c", "o42", "c", "t32", "c", "c", "t42", "c", "c",
+    "o20", "p", "o21", "p", "t10", "p", "o30", "p", "o22", "p", "t20", "p", "t11", "p", "o31", "p", "t30",
+    "p", "o40", "p", "t12", "p", "t40", "t21", "o32", "o41", "t22", "c", "t31", "c", "o42", "c", "t32", "c",
+    "c", "t41", "c", "t42", "c", "c",
 )
 
 

time: 93.1 us -> 91 us (0.977)
  Pallas kernels: 88.8 us -> 86.6 us
    pallas_call x1, Pallas kernels: 88.8 us -> 86.6 us  [per_device(): pl.pallas_call(kernel, out_shape=(jax.ShapeDtypeStruct((3, 32, 64), F32),...]
where the time goes in v3:
time: 91 us; the launch traced here: 90.7 us
  Pallas kernels  86.6 us (95%)
  local copies, waits for them, and re-layouts  3.48 us (4%)
    pallas_call x1, Pallas kernels, per_device(): pl.pallas_call(kernel, out_shape=(jax.ShapeDtypeStruct((3, 32, 64), F32),...  86.6 us
    unnamed x2, local copies, waits for them, and re-layouts  3.48 us

profile of v3, /device:TPU:1, one launch (start us, length us, event | category | flops | bytes accessed | tf_op | source)
XLA Modules:
  0.0 90.7 jit_solution(5208950379293078781)
XLA Ops:
  0.6 86.6 %shard_map.77 = (f32[3,32,64]{2,1,0:T(8,128)}, f32[3,256,256]{2,1,0:T(8,128)}) custom-call(bf16[2,16,64,256]{3,2,1,0:T(8,128)(2,1)} %bitcast.12, bf16[3,2,64,256]{3,2,1,0:T(8,128)(2,1)} %bitcast.14, s32[3]{0:T(128)} %bitcast.16, f32[2,2,256,256]{3,2,1,0:T(8,128)} %bitcast.13, f32[3,2,256,256]{3,2,1,0:T(8,128)} %bitcast.11, f32[2]{0:T(128)} %bitcast.17), custom_call_target="tpu_custom_call" | custom-call | tf_op jit(solution)/shard_map/pallas_call | solution.py:463
  87.3 1.4 %copy.11 = f32[3,1,1,64,32]{3,4,2,1,0:T(8,128)} copy(f32[3,1,1,64,32]{3,4,2,1,0:T(8,128)} %bitcast.15) | data formatting | bytes 49152
  88.7 2.1 %copy.12 = f32[3,256,256]{2,1,0:T(8,128)} copy(f32[3,256,256]{2,1,0:T(8,128)} %get-tuple-element.11) | data formatting | bytes 1572864

commit v4 on v3

--- a/solution.py
+++ b/solution.py
@@ -249,7 +249,8 @@
             each(NQ - 1, lambda i, level=level: send_q(level, 0, i).start())
             for to in range(NQ):
                 sent[level, to, 1] = x_imag[32 * to : 32 * to + 32]
-            each(NQ - 1, lambda i, level=level: send_q(level, 1, i).start())
+            for due in ((0,), (), (1, 2))[level]:
+                each(NQ - 1, lambda i, due=due: send_q(due, 1, i).start())
             if level < 2:
                 yield
                 q_pieces = (q_big[level, 0], q_big[level, 1])
@@ -415,10 +416,11 @@
 
     both(across_z)
     both(across_y)
+    both(back_z)
     panel_sums = [sum_q(level, 1) for level in range(3)] + [jnp.zeros((32, 256), F32)]
     pole_sent[...] = jnp.concatenate(panel_sums, axis=0).T.reshape(NP, 32, 128)
     each(NP - 1, lambda i: send_p(i).start())
-    both(back_z)
+    both(back_x)
     each(NP - 1, wait_p)
     pole_got[pole] = pole_sent[pole]
     for half in range(NC):
@@ -427,7 +429,6 @@
             total = total + pole_got[layer * NC + half]
         for level in range(3):
             panel_out[level, :, 32 * half : 32 * half + 32] = total[:, 32 * level : 32 * level + 32]
-    both(back_x)
     both(back_core)
     both(place_diag)
 

time: 91 us -> 90.1 us (level)
  no operation moved by 1% of the time
where the time goes in v4:
time: 90.1 us; the launch traced here: 89.9 us
  Pallas kernels  85.8 us (95%)
  local copies, waits for them, and re-layouts  3.48 us (4%)
    pallas_call x1, Pallas kernels, per_device(): pl.pallas_call(kernel, out_shape=(jax.ShapeDtypeStruct((3, 32, 64), F32),...  85.8 us
    unnamed x2, local copies, waits for them, and re-layouts  3.48 us

profile of v4, /device:TPU:1, one launch (start us, length us, event | category | flops | bytes accessed | tf_op | source)
XLA Modules:
  0.0 89.9 jit_solution(11035727109009812435)
XLA Ops:
  0.6 85.8 %shard_map.77 = (f32[3,32,64]{2,1,0:T(8,128)}, f32[3,256,256]{2,1,0:T(8,128)}) custom-call(bf16[2,16,64,256]{3,2,1,0:T(8,128)(2,1)} %bitcast.12, bf16[3,2,64,256]{3,2,1,0:T(8,128)(2,1)} %bitcast.14, s32[3]{0:T(128)} %bitcast.16, f32[2,2,256,256]{3,2,1,0:T(8,128)} %bitcast.13, f32[3,2,256,256]{3,2,1,0:T(8,128)} %bitcast.11, f32[2]{0:T(128)} %bitcast.17), custom_call_target="tpu_custom_call" | custom-call | tf_op jit(solution)/shard_map/pallas_call | solution.py:464
  86.4 1.4 %copy.11 = f32[3,1,1,64,32]{3,4,2,1,0:T(8,128)} copy(f32[3,1,1,64,32]{3,4,2,1,0:T(8,128)} %bitcast.15) | data formatting | bytes 49152
  87.8 2.1 %copy.12 = f32[3,256,256]{2,1,0:T(8,128)} copy(f32[3,256,256]{2,1,0:T(8,128)} %get-tuple-element.11) | data formatting | bytes 1572864
